TPU v7x, 256 devices: a whole 4x4x8 slice. The times are simulated.
256 devices in a mesh: row: 16 (over y, x), col: 16 (over z, core).
Axes of the slice: x: 4, y: 4, z: 8, core: 2. Of those that a mesh axis runs over, the one named last changes fastest.
Arguments:
- block_values: float32 [16, 16, 40, 128, 128], P('row', 'col'), may hold values from 7.8125e-06 to 0.00078125
- block_index: int32 [16, 16, 2, 40], P('row', 'col'), may hold values from 0 to 31, as said below
- block_count: int32 [16, 16], P('row', 'col'), may hold values from 1 to 40, as said below
- strength: float32 [32], replicated, may hold values from 1 to 30
- raw_scores: float32 [512, 32, 128], P(('row', 'col')), may hold values from -24 to 24
Outputs:
- smoothed: float32 [512, 32, 128], P(('row', 'col'))
- final_residual: float32 [512, 32, 128], P(('row', 'col'))
Inputs may be any that keep to these rules, and one draw needn't show every extreme that they name: `block_count`: some device has exactly 40 live slots; the others hold between half and all of their share of the upper triangle, scaled to 40. `block_index`: the live slots of one device name distinct blocks, each with global block row at most its global block column; slots at or above the count hold pairs in range that are ignored.
All inputs are finite; a program needn't handle non-finite values.
Results may differ from a plain program's by a relative error of at most 0.0003.
Values sent between devices are 32-bit elements; how exact they have to be, the bound alone decides.
A program may use at most 64 MiB of HBM per device.

v0:
```python
import jax
import jax.numpy as jnp
from jax import lax
from jax.sharding import PartitionSpec as P

ITERS = 3


def local_terms(values, row_index, col_index, panel_rows, panel_cols):
    picked_cols = jnp.take(panel_cols, col_index, axis=0)
    picked_rows = jnp.take(panel_rows, row_index, axis=0)
    to_rows = jnp.einsum("crk,cik->cri", picked_cols, values, precision=lax.Precision.HIGHEST)
    to_cols = jnp.einsum("cri,cik->crk", picked_rows, values, precision=lax.Precision.HIGHEST)
    row_part = jax.ops.segment_sum(to_rows, row_index, num_segments=panel_rows.shape[0])
    col_part = jax.ops.segment_sum(to_cols, col_index, num_segments=panel_cols.shape[0])
    return (row_part, col_part)


def fold_terms(row_part, col_part):
    return lax.psum_scatter(row_part, "col", scatter_dimension=0, tiled=True) + lax.psum_scatter(
        col_part, "row", scatter_dimension=0, tiled=True
    )


def total(field):
    return jnp.sum(field, axis=(0, 2))


def global_sum(partial_sum):
    return lax.psum(partial_sum, ("row", "col"))


def shards(block_values, block_index, block_count, strength, raw_scores):
    values = block_values[0, 0]
    row_index = block_index[0, 0, 0]
    col_index = block_index[0, 0, 1]
    live_mask = (jnp.arange(values.shape[0], dtype=jnp.int32) < block_count[0, 0]).astype(
        jnp.float32
    )
    masked = values * live_mask[:, None, None]
    segment = raw_scores.shape[0]
    block_size = raw_scores.shape[2]
    rows_here = lax.axis_size("col") * segment
    cols_here = lax.axis_size("row") * segment
    ones_rows = jnp.ones((rows_here, 1, block_size), jnp.float32)
    ones_cols = jnp.ones((cols_here, 1, block_size), jnp.float32)
    degree_rows, degree_cols = local_terms(masked, row_index, col_index, ones_rows, ones_cols)
    degree = fold_terms(degree_rows, degree_cols)
    gains = strength[None, :, None]
    smoothed = jnp.zeros_like(raw_scores)
    residual = raw_scores
    direction = raw_scores
    norm_now = global_sum(total(residual * residual))
    for iteration in range(ITERS):
        panel_rows = lax.all_gather(direction, "col", axis=0, tiled=True)
        panel_cols = lax.all_gather(direction, "row", axis=0, tiled=True)
        row_part, col_part = local_terms(masked, row_index, col_index, panel_rows, panel_cols)
        product = fold_terms(row_part, col_part)
        image = direction + gains * (degree * direction - product)
        step_size = norm_now / global_sum(total(direction * image))
        smoothed = smoothed + step_size[None, :, None] * direction
        residual = residual - step_size[None, :, None] * image
        norm_next = global_sum(total(residual * residual))
        direction = residual + (norm_next / norm_now)[None, :, None] * direction
        norm_now = norm_next
    return (smoothed, residual)


def solution(mesh):
    placed = (
        P("row", "col", None, None, None),
        P("row", "col", None, None),
        P("row", "col"),
        P(),
        P(("row", "col"), None, None),
    )
    return jax.shard_map(
        shards,
        mesh=mesh,
        in_specs=placed,
        out_specs=(P(("row", "col"), None, None), P(("row", "col"), None, None)),
        check_vma=False,
    )
```

profile of v0, /device:TPU:1, one launch (start us, length us, event | category | flops | bytes accessed | tf_op | source)
XLA Modules:
  0.0 916.9 jit_solution(5695150841030016190)
XLA Ops:
  9.4 23.0 %all_gather.19 = f32[32,32,128]{2,1,0:T(8,128)S(1)} all-gather(f32[2,32,128]{2,1,0:T(8,128)} %param.13), channel_id=1, replica_groups=mesh['row'=16,'col'=16] {'col'}, dimensions={0}, use_global_device_ids=true | all-gather | bytes 557056 | tf_op jit(solution)/shard_map/all_gather | solution.py:55
  33.0 5.0 fusion.4
  38.1 4.9 scatter_fusion.1
  43.9 19.6 %all_gather.18 = f32[32,32,128]{2,1,0:T(8,128)S(1)} all-gather(f32[2,32,128]{2,1,0:T(8,128)S(1)} %copy-done.7), channel_id=1, replica_groups=mesh['row'=16,'col'=16] {'row'}, dimensions={0}, use_global_device_ids=true | all-gather | bytes 557056 | tf_op jit(solution)/shard_map/all_gather | solution.py:56
  64.9 6.2 fusion.5
  71.1 4.7 scatter_fusion
  80.5 4.3 fusion.7
  85.7 2.3 fusion.6
  88.7 58.4 %all-reduce.1 = f32[32,1,128]{2,0,1:T(8,128)S(1)} all-reduce(f32[32,1,128]{2,0,1:T(8,128)S(1)} %bitcast.49), channel_id=3, replica_groups=mesh['row'=16,'col'=16] {'row'}, use_global_device_ids=true, to_apply=%region_5.7.clone | all-reduce | flops 4096 | bytes 32768
  147.1 61.3 %all-reduce = f32[32,1,128]{2,0,1:T(8,128)S(1)} all-reduce(f32[32,1,128]{2,0,1:T(8,128)S(1)} %bitcast.48), channel_id=2, replica_groups=mesh['row'=16,'col'=16] {'col'}, use_global_device_ids=true, to_apply=%region_3.5.clone | all-reduce | flops 4096 | bytes 32768
  209.5 74.0 %all-reduce.2 = (f32[32]{0:T(128)S(1)}, f32[32]{0:T(128)S(1)}) all-reduce(f32[32]{0:T(128)S(1)} %get-tuple-element.5, f32[32]{0:T(128)S(1)} %get-tuple-element.4), channel_id=1, replica_groups=mesh['row'=16,'col'=16] {'row','col'}, use_global_device_ids=true, to_apply=%region_1.2 | all-reduce | flops 64 | bytes 512 | tf_op jit(solution)/shard_map/psum | solution.py:30
  284.5 74.5 %psum.44 = f32[32]{0:T(128)S(1)} all-reduce(f32[32]{0:T(128)S(1)} %get-tuple-element.10), channel_id=1, replica_groups=mesh['row'=16,'col'=16] {'row','col'}, use_global_device_ids=true, to_apply=%region_13.16 | all-reduce | flops 32 | bytes 256 | tf_op jit(solution)/shard_map/psum | solution.py:30
  359.0 17.2 %all_gather.21 = f32[32,32,128]{2,1,0:T(8,128)S(1)} all-gather(f32[2,32,128]{2,1,0:T(8,128)S(1)} %multiply_add_fusion.4), channel_id=1, replica_groups=mesh['row'=16,'col'=16] {'col'}, dimensions={0}, use_global_device_ids=true | all-gather | bytes 557056 | tf_op jit(solution)/shard_map/all_gather | solution.py:55
  377.7 4.3 fusion.2
  382.1 4.7 scatter_fusion.3
  387.7 19.2 %all_gather.20 = f32[32,32,128]{2,1,0:T(8,128)S(1)} all-gather(f32[2,32,128]{2,1,0:T(8,128)S(1)} %multiply_add_fusion.4), channel_id=1, replica_groups=mesh['row'=16,'col'=16] {'row'}, dimensions={0}, use_global_device_ids=true | all-gather | bytes 557056 | tf_op jit(solution)/shard_map/all_gather | solution.py:56
  408.3 6.2 fusion.3
  414.5 4.7 scatter_fusion.2
  420.1 38.4 %reduce-scatter.15.cloned.1.call-done = f32[2,32,128]{2,1,0:T(8,128)} async-done(((f32[32,32,128]{2,1,0:T(8,128)}), f32[2,32,128]{2,1,0:T(8,128)}) %reduce-scatter.15.cloned.1.call-update) | async-done | bytes 32784 | tf_op jit(solution)/shard_map/reduce_scatter | solution.py:20
  458.5 57.2 %reduce-scatter.13.cloned.1.call-done = f32[2,32,128]{2,1,0:T(8,128)} async-done(((f32[32,32,128]{2,1,0:T(8,128)}), f32[2,32,128]{2,1,0:T(8,128)}) %reduce-scatter.13.cloned.1.call-update) | async-done | bytes 32784 | tf_op jit(solution)/shard_map/reduce_scatter | solution.py:20
  516.7 79.6 %psum.45 = f32[32]{0:T(128)S(1)} all-reduce(f32[32]{0:T(128)S(1)} %multiply_reduce_fusion.2), channel_id=1, replica_groups=mesh['row'=16,'col'=16] {'row','col'}, use_global_device_ids=true, to_apply=%region_19.22 | all-reduce | flops 32 | bytes 256 | tf_op jit(solution)/shard_map/psum | solution.py:30
  597.2 72.4 %psum.46 = f32[32]{0:T(128)S(1)} all-reduce(f32[32]{0:T(128)S(1)} %get-tuple-element.8), channel_id=1, replica_groups=mesh['row'=16,'col'=16] {'row','col'}, use_global_device_ids=true, to_apply=%region_21.24 | all-reduce | flops 32 | bytes 256 | tf_op jit(solution)/shard_map/psum | solution.py:30
  669.6 18.1 %all_gather.23 = f32[32,32,128]{2,1,0:T(8,128)S(1)} all-gather(f32[2,32,128]{2,1,0:T(8,128)S(1)} %multiply_add_fusion.2), channel_id=1, replica_groups=mesh['row'=16,'col'=16] {'col'}, dimensions={0}, use_global_device_ids=true | all-gather | bytes 557056 | tf_op jit(solution)/shard_map/all_gather | solution.py:55
  689.2 4.3 fusion
  693.6 4.7 scatter_fusion.5
  699.1 19.2 %all_gather.22 = f32[32,32,128]{2,1,0:T(8,128)S(1)} all-gather(f32[2,32,128]{2,1,0:T(8,128)S(1)} %multiply_add_fusion.2), channel_id=1, replica_groups=mesh['row'=16,'col'=16] {'row'}, dimensions={0}, use_global_device_ids=true | all-gather | bytes 557056 | tf_op jit(solution)/shard_map/all_gather | solution.py:56
  719.8 5.3 fusion.1
  725.2 2.7 scatter_fusion.4
  728.7 41.8 %reduce-scatter.19.cloned.1.call-done = f32[2,32,128]{2,1,0:T(8,128)} async-done(((f32[32,32,128]{2,1,0:T(8,128)}), f32[2,32,128]{2,1,0:T(8,128)}) %reduce-scatter.19.cloned.1.call-update) | async-done | bytes 32784 | tf_op jit(solution)/shard_map/reduce_scatter | solution.py:20
  770.5 57.3 %reduce-scatter.17.cloned.1.call-done = f32[2,32,128]{2,1,0:T(8,128)} async-done(((f32[32,32,128]{2,1,0:T(8,128)}), f32[2,32,128]{2,1,0:T(8,128)}) %reduce-scatter.17.cloned.1.call-update) | async-done | bytes 32784 | tf_op jit(solution)/shard_map/reduce_scatter | solution.py:20
  828.8 79.8 %psum.47 = f32[32]{0:T(128)S(1)} all-reduce(f32[32]{0:T(128)S(1)} %multiply_reduce_fusion), channel_id=1, replica_groups=mesh['row'=16,'col'=16] {'row','col'}, use_global_device_ids=true, to_apply=%region_27.30 | all-reduce | flops 32 | bytes 256 | tf_op jit(solution)/shard_map/psum | solution.py:30
  908.5 1.5 multiply_subtract_fusion
  (74 shorter events, 23.8 us)
Async XLA Ops:
  7.2 201.3 %reduce-scatter.11.cloned.1.call-start = ((), (), s32[]{:S(2)}) async-start(), calls=%async_computation.7 | async-start | bytes 557056 | tf_op jit(solution)/shard_map/reduce_scatter | solution.py:20
  33.0 10.9 %copy-start.7 = (f32[2,32,128]{2,1,0:T(8,128)S(1)}, f32[2,32,128]{2,1,0:T(8,128)}, u32[]{:S(2)}) copy-start(f32[2,32,128]{2,1,0:T(8,128)} %param.13) | copy-start | bytes 98308
  38.0 26.9 %copy-start = (f32[1,1,40,128,128]{4,3,2,1,0:T(8,128)S(1)}, f32[1,1,40,128,128]{4,3,2,1,0:T(8,128)}, u32[]{:S(2)}) copy-start(f32[1,1,40,128,128]{4,3,2,1,0:T(8,128)} %param.9) | copy-start | bytes 7864324
  42.9 0.8 copy-start.3
  43.8 164.7 %reduce-scatter.9.cloned.1.call-start = ((), (), s32[]{:S(2)}) async-start(), calls=%async_computation.6 | async-start | bytes 557056 | tf_op jit(solution)/shard_map/reduce_scatter | solution.py:20
  71.1 6.8 copy-start.10
  71.1 7.4 copy-start.9
  75.8 0.8 copy-start.4
  76.7 381.8 %reduce-scatter.15.cloned.1.call-start = ((), (), s32[]{:S(2)}) async-start(), calls=%async_computation.9 | async-start | bytes 557056 | tf_op jit(solution)/shard_map/reduce_scatter | solution.py:20
  80.4 128.1 %copy-start.8 = (f32[32]{0:T(128)S(1)}, f32[32]{0:T(128)}, u32[]{:S(2)}) copy-start(f32[32]{0:T(128)} %param.12) | copy-start | bytes 388
  386.8 0.8 copy-start.5
  387.6 128.1 %reduce-scatter.13.cloned.1.call-start = ((), (), s32[]{:S(2)}) async-start(), calls=%async_computation.8 | async-start | bytes 557056 | tf_op jit(solution)/shard_map/reduce_scatter | solution.py:20
  419.2 0.8 copy-start.6
  420.0 350.5 %reduce-scatter.19.cloned.1.call-start = ((), (), s32[]{:S(2)}) async-start(), calls=%async_computation.11 | async-start | bytes 557056 | tf_op jit(solution)/shard_map/reduce_scatter | solution.py:20
  698.3 0.8 copy-start.2
  699.1 128.7 %reduce-scatter.17.cloned.1.call-start = ((), (), s32[]{:S(2)}) async-start(), calls=%async_computation.10 | async-start | bytes 557056 | tf_op jit(solution)/shard_map/reduce_scatter | solution.py:20
  727.9 0.8 copy-start.1
Sparse Core Ops, SparseCore 0:
  43.9 73.4 reduce-scatter.10
  120.0 55.2 reduce-scatter.8
  387.7 70.6 reduce-scatter.14
  461.0 54.6 reduce-scatter.12
  699.2 71.2 reduce-scatter.18
  773.0 54.7 reduce-scatter.16
where the time goes:
time: 918 us; the launch traced here: 917 us
  blocking collectives  616 us (67%)
  waiting for transfers between devices  195 us (21%)
  matrix products  37.9 us (4%)
  other arithmetic  35.4 us (4%)
  between operations  16.3 us (2%)
  local copies, waits for them, and re-layouts  15.9 us (2%)
    psum x5, blocking collectives, global_sum(): return lax.psum(partial_sum, ('row', 'col'))  380 us
    unnamed x2, blocking collectives  120 us
    reduce_scatter x3, waiting for transfers between devices, fold_terms(): lax.psum_scatter(row_part, 'col', scatter_dimension=0, tiled=True)  115 us
    reduce_scatter x3, waiting for transfers between devices, fold_terms(): lax.psum_scatter(col_part, 'row', scatter_dimension=0, tiled=True)  80.2 us
    all_gather x3, blocking collectives, shards(): panel_rows = lax.all_gather(direction, 'col', axis=0, tiled=True)  58.3 us
    all_gather x3, blocking collectives, shards(): panel_cols = lax.all_gather(direction, 'row', axis=0, tiled=True)  58 us
    dot_general x4, matrix products, local_terms(): jnp.einsum('crk,cik->cri', picked_cols, values, precision=lax.Precision.H...  22 us
  transfers between devices with their start and end apart: 6, of which 4 were waited for; matrix products, arithmetic and copies ran while one was open for 5% of the time, Pallas kernels for 0%

commit v1 on v0

--- a/solution.py
+++ b/solution.py
@@ -4,6 +4,12 @@
 from jax.sharding import PartitionSpec as P
 
 ITERS = 3
+
+
+def in_order(parts, dim):
+    parts = jnp.moveaxis(parts, 0, dim)
+    shape = parts.shape
+    return parts.reshape(*shape[:dim], shape[dim] * shape[dim + 1], *shape[dim + 2 :])
 
 
 def local_terms(values, row_index, col_index, panel_rows, panel_cols):
@@ -53,7 +59,19 @@
     norm_now = global_sum(total(residual * residual))
     for iteration in range(ITERS):
         panel_rows = lax.all_gather(direction, "col", axis=0, tiled=True)
-        panel_cols = lax.all_gather(direction, "row", axis=0, tiled=True)
+        size = lax.axis_size("row")
+        pairs = [(i, (i + 1) % size) for i in range(size)]
+        back = [(b, a) for a, b in pairs]
+        lower, upper = ([], [])
+        for step in range(size - 1):
+            if step % 2 == 0:
+                lower.append(lax.ppermute(lower[-1] if lower else direction, "row", pairs))
+            else:
+                upper.append(lax.ppermute(upper[-1] if upper else direction, "row", back))
+        parts = jnp.stack([*lower[::-1], direction, *upper])
+        shift = lax.axis_index("row") - len(lower)
+        parts = parts[(jnp.arange(size) - shift) % size]
+        panel_cols = in_order(parts, 0)
         row_part, col_part = local_terms(masked, row_index, col_index, panel_rows, panel_cols)
         product = fold_terms(row_part, col_part)
         image = direction + gains * (degree * direction - product)

time: 918 us -> 1070 us (1.17); the launches traced: 917 us -> 1060 us
  starting transfers between devices: 0.25 us -> 106 us
  blocking collectives: 616 us -> 571 us
  local copies, waits for them, and re-layouts: 15.9 us -> 59.7 us
  waiting for transfers between devices: 195 us -> 230 us
    ppermute x0 -> x45, starting transfers between devices: none -> 106 us  [the longest x21 101 us: shards(): upper.append(lax.ppermute(upper[-1] if upper else direction, 'row', back))]
    all_gather x3 -> x0, blocking collectives: 58 us -> none  [shards(): panel_cols = lax.all_gather(direction, 'row', axis=0, tiled=True)]
    unnamed x24 -> x107, local copies, waits for them, and re-layouts: 5.96 us -> 43 us
    ppermute x0 -> x45, waiting for transfers between devices: none -> 32.7 us  [the longest x24 30.1 us: shards(): lower.append(lax.ppermute(lower[-1] if lower else direction, 'row', pairs))]
    all_gather x3, blocking collectives: 58.3 us -> 71.6 us  [shards(): panel_rows = lax.all_gather(direction, 'col', axis=0, tiled=True)]
  transfers between devices with their start and end apart: 6 -> 51, of which waited for: 4 -> 23; matrix products, arithmetic and copies ran while one was open for 5% -> 11% of each run, Pallas kernels for 0% -> 0%
where the time goes in v1:
time: 1070 us; the launch traced here: 1060 us
  blocking collectives  571 us (53%)
  waiting for transfers between devices  230 us (21%)
  starting transfers between devices  106 us (10%)
  local copies, waits for them, and re-layouts  59.7 us (6%)
  matrix products  38 us (4%)
  other arithmetic  35.9 us (3%)
  between operations  17.1 us (2%)
    psum x5, blocking collectives, global_sum(): return lax.psum(partial_sum, ('row', 'col'))  381 us
    unnamed x2, blocking collectives  119 us
    reduce_scatter x3, waiting for transfers between devices, fold_terms(): lax.psum_scatter(row_part, 'col', scatter_dimension=0, tiled=True)  114 us
    ppermute x21, starting transfers between devices, shards(): upper.append(lax.ppermute(upper[-1] if upper else direction, 'row', back))  101 us
    reduce_scatter x3, waiting for transfers between devices, fold_terms(): lax.psum_scatter(col_part, 'row', scatter_dimension=0, tiled=True)  83.1 us
    all_gather x3, blocking collectives, shards(): panel_rows = lax.all_gather(direction, 'col', axis=0, tiled=True)  71.6 us
    unnamed x107, local copies, waits for them, and re-layouts  43 us
    ppermute x24, waiting for transfers between devices, shards(): lower.append(lax.ppermute(lower[-1] if lower else direction, 'row', pairs))  30.1 us
  transfers between devices with their start and end apart: 51, of which 23 were waited for; matrix products, arithmetic and copies ran while one was open for 11% of the time, Pallas kernels for 0%

profile of v1, /device:TPU:1, one launch (start us, length us, event | category | flops | bytes accessed | tf_op | source)
XLA Modules:
  0.0 1057.9 jit_solution(17116977009839217490)
XLA Ops:
  13.1 22.5 %all_gather.9 = f32[32,32,128]{2,1,0:T(8,128)S(1)} all-gather(f32[2,32,128]{2,1,0:T(8,128)} %param.13), channel_id=1, replica_groups=mesh['row'=16,'col'=16] {'col'}, dimensions={0}, use_global_device_ids=true | all-gather | bytes 557056 | tf_op jit(solution)/shard_map/all_gather | solution.py:61
  37.2 5.4 collective-permute-done.1
  43.2 4.9 collective-permute-start.9
  48.6 5.0 fusion.4
  58.5 4.9 scatter_fusion.1
  64.3 4.8 collective-permute-start.11
  70.2 5.1 collective-permute-start.12
  76.3 5.1 collective-permute-start.13
  82.4 5.1 collective-permute-start.14
  100.6 6.2 fusion.5
  124.8 55.8 %all-reduce.1 = f32[32,1,128]{2,0,1:T(8,128)S(1)} all-reduce(f32[32,1,128]{2,0,1:T(8,128)S(1)} %bitcast.153), channel_id=3, replica_groups=mesh['row'=16,'col'=16] {'row'}, use_global_device_ids=true, to_apply=%region_5.7.clone | all-reduce | flops 4096 | bytes 32768
  180.6 63.0 %all-reduce = f32[32,1,128]{2,0,1:T(8,128)S(1)} all-reduce(f32[32,1,128]{2,0,1:T(8,128)S(1)} %bitcast.152), channel_id=2, replica_groups=mesh['row'=16,'col'=16] {'col'}, use_global_device_ids=true, to_apply=%region_3.5.clone | all-reduce | flops 4096 | bytes 32768
  244.6 74.0 %all-reduce.2 = (f32[32]{0:T(128)S(1)}, f32[32]{0:T(128)S(1)}) all-reduce(f32[32]{0:T(128)S(1)} %get-tuple-element.5, f32[32]{0:T(128)S(1)} %get-tuple-element.4), channel_id=1, replica_groups=mesh['row'=16,'col'=16] {'row','col'}, use_global_device_ids=true, to_apply=%region_1.2 | all-reduce | flops 64 | bytes 512 | tf_op jit(solution)/shard_map/psum | solution.py:36
  319.6 74.4 %psum.44 = f32[32]{0:T(128)S(1)} all-reduce(f32[32]{0:T(128)S(1)} %get-tuple-element.10), channel_id=1, replica_groups=mesh['row'=16,'col'=16] {'row','col'}, use_global_device_ids=true, to_apply=%region_13.16 | all-reduce | flops 32 | bytes 256 | tf_op jit(solution)/shard_map/psum | solution.py:36
  395.8 5.0 collective-permute-done.15
  431.5 24.1 %all_gather.10 = f32[32,32,128]{2,1,0:T(8,128)S(1)} all-gather(f32[2,32,128]{2,1,0:T(8,128)S(1)} %multiply_add_fusion.4), channel_id=1, replica_groups=mesh['row'=16,'col'=16] {'col'}, dimensions={0}, use_global_device_ids=true | all-gather | bytes 557056 | tf_op jit(solution)/shard_map/all_gather | solution.py:61
  457.1 5.1 collective-permute-start.28
  466.6 4.8 scatter_fusion.3
  472.3 4.9 collective-permute-start.29
  494.1 6.2 fusion.3
  505.9 39.9 %reduce-scatter.15.cloned.1.call-done = f32[2,32,128]{2,1,0:T(8,128)} async-done(((f32[32,32,128]{2,1,0:T(8,128)}), f32[2,32,128]{2,1,0:T(8,128)}) %reduce-scatter.15.cloned.1.call-update) | async-done | bytes 32784 | tf_op jit(solution)/shard_map/reduce_scatter | solution.py:26
  545.8 57.2 %reduce-scatter.13.cloned.1.call-done = f32[2,32,128]{2,1,0:T(8,128)} async-done(((f32[32,32,128]{2,1,0:T(8,128)}), f32[2,32,128]{2,1,0:T(8,128)}) %reduce-scatter.13.cloned.1.call-update) | async-done | bytes 32784 | tf_op jit(solution)/shard_map/reduce_scatter | solution.py:26
  604.0 80.0 %psum.45 = f32[32]{0:T(128)S(1)} all-reduce(f32[32]{0:T(128)S(1)} %multiply_reduce_fusion.2), channel_id=1, replica_groups=mesh['row'=16,'col'=16] {'row','col'}, use_global_device_ids=true, to_apply=%region_19.22 | all-reduce | flops 32 | bytes 256 | tf_op jit(solution)/shard_map/psum | solution.py:36
  684.9 72.3 %psum.46 = f32[32]{0:T(128)S(1)} all-reduce(f32[32]{0:T(128)S(1)} %get-tuple-element.8), channel_id=1, replica_groups=mesh['row'=16,'col'=16] {'row','col'}, use_global_device_ids=true, to_apply=%region_21.24 | all-reduce | flops 32 | bytes 256 | tf_op jit(solution)/shard_map/psum | solution.py:36
  758.5 5.5 collective-permute-done.30
  794.5 25.0 %all_gather.11 = f32[32,32,128]{2,1,0:T(8,128)S(1)} all-gather(f32[2,32,128]{2,1,0:T(8,128)S(1)} %multiply_add_fusion.2), channel_id=1, replica_groups=mesh['row'=16,'col'=16] {'col'}, dimensions={0}, use_global_device_ids=true | all-gather | bytes 557056 | tf_op jit(solution)/shard_map/all_gather | solution.py:61
  821.1 5.1 collective-permute-start.43
  836.5 4.8 collective-permute-start.44
  859.1 5.3 fusion.1
  867.9 43.2 %reduce-scatter.19.cloned.1.call-done = f32[2,32,128]{2,1,0:T(8,128)} async-done(((f32[32,32,128]{2,1,0:T(8,128)}), f32[2,32,128]{2,1,0:T(8,128)}) %reduce-scatter.19.cloned.1.call-update) | async-done | bytes 32784 | tf_op jit(solution)/shard_map/reduce_scatter | solution.py:26
  911.1 57.1 %reduce-scatter.17.cloned.1.call-done = f32[2,32,128]{2,1,0:T(8,128)} async-done(((f32[32,32,128]{2,1,0:T(8,128)}), f32[2,32,128]{2,1,0:T(8,128)}) %reduce-scatter.17.cloned.1.call-update) | async-done | bytes 32784 | tf_op jit(solution)/shard_map/reduce_scatter | solution.py:26
  969.1 79.9 %psum.47 = f32[32]{0:T(128)S(1)} all-reduce(f32[32]{0:T(128)S(1)} %multiply_reduce_fusion), channel_id=1, replica_groups=mesh['row'=16,'col'=16] {'row','col'}, use_global_device_ids=true, to_apply=%region_27.30 | all-reduce | flops 32 | bytes 256 | tf_op jit(solution)/shard_map/psum | solution.py:36
  (252 shorter events, 179.3 us)
Async XLA Ops:
  7.2 236.5 %reduce-scatter.11.cloned.1.call-start = ((), (), s32[]{:S(2)}) async-start(), calls=%async_computation.7 | async-start | bytes 557056 | tf_op jit(solution)/shard_map/reduce_scatter | solution.py:26
  7.2 29.2 %collective-permute-start = (f32[2,32,128]{2,1,0:T(8,128)}, f32[2,32,128]{2,1,0:T(8,128)S(1)}, u32[]{:S(2)}, u32[]{:S(2)}) collective-permute-start(f32[2,32,128]{2,1,0:T(8,128)} %param.13), channel_id=1, source_target_pairs={{0,16},{16,32},{32,48},{48,64},{64,80},{80,96},{96,112},{112,128},... | collective-permute-start | bytes 98312 | tf_op jit(solution)/shard_map/ppermute | solution.py:68
  9.3 33.8 %collective-permute-start.8 = (f32[2,32,128]{2,1,0:T(8,128)}, f32[2,32,128]{2,1,0:T(8,128)S(1)}, u32[]{:S(2)}, u32[]{:S(2)}) collective-permute-start(f32[2,32,128]{2,1,0:T(8,128)} %param.13), channel_id=1, source_target_pairs={{16,0},{32,16},{48,32},{64,48},{80,64},{96,80},{112,96},{128,112},... | collective-permute-start | bytes 98312 | tf_op jit(solution)/shard_map/ppermute | solution.py:70
  36.4 6.2 collective-permute-start.1
  43.2 10.5 collective-permute-start.9
  48.6 9.8 collective-permute-start.3
  53.6 10.7 %collective-permute-start.10 = (f32[2,32,128]{2,1,0:T(8,128)S(1)}, f32[2,32,128]{2,1,0:T(8,128)S(1)}, u32[]{:S(2)}, u32[]{:S(2)}) collective-permute-start(f32[2,32,128]{2,1,0:T(8,128)S(1)} %collective-permute-done.9), channel_id=1, source_target_pairs={{16,0},{32,16},{48,32},{64,48},{80,64},{96,80},{112,96},{128,112},... | collective-permute-start | bytes 98312 | tf_op jit(solution)/shard_map/ppermute | solution.py:70
  58.4 10.8 %collective-permute-start.4 = (f32[2,32,128]{2,1,0:T(8,128)S(1)}, f32[2,32,128]{2,1,0:T(8,128)S(1)}, u32[]{:S(2)}, u32[]{:S(2)}) collective-permute-start(f32[2,32,128]{2,1,0:T(8,128)S(1)} %collective-permute-done.3), channel_id=1, source_target_pairs={{0,16},{16,32},{32,48},{48,64},{64,80},{80,96},{96,112},{112,128},... | collective-permute-start | bytes 98312 | tf_op jit(solution)/shard_map/ppermute | solution.py:68
  64.3 179.4 %reduce-scatter.9.cloned.1.call-start = ((), (), s32[]{:S(2)}) async-start(), calls=%async_computation.6 | async-start | bytes 557056 | tf_op jit(solution)/shard_map/reduce_scatter | solution.py:26
  75.3 6.3 collective-permute-start.6
  81.6 6.1 collective-permute-start.7
  82.4 14.5 %collective-permute-start.14 = (f32[2,32,128]{2,1,0:T(8,128)S(1)}, f32[2,32,128]{2,1,0:T(8,128)S(1)}, u32[]{:S(2)}, u32[]{:S(2)}) collective-permute-start(f32[2,32,128]{2,1,0:T(8,128)S(1)} %collective-permute-done.13), channel_id=1, source_target_pairs={{16,0},{32,16},{48,32},{64,48},{80,64},{96,80},{112,96},{128,112},... | collective-permute-start | bytes 98312 | tf_op jit(solution)/shard_map/ppermute | solution.py:70
  112.3 433.5 %reduce-scatter.15.cloned.1.call-start = ((), (), s32[]{:S(2)}) async-start(), calls=%async_computation.9 | async-start | bytes 557056 | tf_op jit(solution)/shard_map/reduce_scatter | solution.py:26
  394.7 6.1 collective-permute-start.15
  400.8 6.1 collective-permute-start.23
  419.0 6.2 collective-permute-start.26
  425.1 6.3 collective-permute-start.20
  425.3 31.8 %collective-permute-start.27 = (f32[2,32,128]{2,1,0:T(8,128)S(1)}, f32[2,32,128]{2,1,0:T(8,128)S(1)}, u32[]{:S(2)}, u32[]{:S(2)}) collective-permute-start(f32[2,32,128]{2,1,0:T(8,128)S(1)} %collective-permute-done.26), channel_id=1, source_target_pairs={{16,0},{32,16},{48,32},{64,48},{80,64},{96,80},{112,96},{128,112},... | collective-permute-start | bytes 98312 | tf_op jit(solution)/shard_map/ppermute | solution.py:70
  431.4 30.7 %collective-permute-start.21 = (f32[2,32,128]{2,1,0:T(8,128)}, f32[2,32,128]{2,1,0:T(8,128)}, u32[]{:S(2)}, u32[]{:S(2)}) collective-permute-start(f32[2,32,128]{2,1,0:T(8,128)} %collective-permute-done.20), channel_id=1, source_target_pairs={{0,16},{16,32},{32,48},{48,64},{64,80},{80,96},{96,112},{112,128},... | collective-permute-start | bytes 98312 | tf_op jit(solution)/shard_map/ppermute | solution.py:68
  457.1 15.2 %collective-permute-start.28 = (f32[2,32,128]{2,1,0:T(8,128)S(1)}, f32[2,32,128]{2,1,0:T(8,128)}, u32[]{:S(2)}, u32[]{:S(2)}) collective-permute-start(f32[2,32,128]{2,1,0:T(8,128)S(1)} %collective-permute-done.27), channel_id=1, source_target_pairs={{16,0},{32,16},{48,32},{64,48},{80,64},{96,80},{112,96},{128,112},... | collective-permute-start | bytes 98312 | tf_op jit(solution)/shard_map/ppermute | solution.py:70
  462.2 15.0 %collective-permute-start.22 = (f32[2,32,128]{2,1,0:T(8,128)}, f32[2,32,128]{2,1,0:T(8,128)}, u32[]{:S(2)}, u32[]{:S(2)}) collective-permute-start(f32[2,32,128]{2,1,0:T(8,128)} %collective-permute-done.21), channel_id=1, source_target_pairs={{0,16},{16,32},{32,48},{48,64},{64,80},{80,96},{96,112},{112,128},... | collective-permute-start | bytes 98312 | tf_op jit(solution)/shard_map/ppermute | solution.py:68
  472.2 130.8 %reduce-scatter.13.cloned.1.call-start = ((), (), s32[]{:S(2)}) async-start(), calls=%async_computation.8 | async-start | bytes 557056 | tf_op jit(solution)/shard_map/reduce_scatter | solution.py:26
  472.3 17.8 %collective-permute-start.29 = (f32[2,32,128]{2,1,0:T(8,128)}, f32[2,32,128]{2,1,0:T(8,128)S(1)}, u32[]{:S(2)}, u32[]{:S(2)}) collective-permute-start(f32[2,32,128]{2,1,0:T(8,128)} %collective-permute-done.28), channel_id=1, source_target_pairs={{16,0},{32,16},{48,32},{64,48},{80,64},{96,80},{112,96},{128,112},... | collective-permute-start | bytes 98312 | tf_op jit(solution)/shard_map/ppermute | solution.py:70
  505.9 405.3 %reduce-scatter.19.cloned.1.call-start = ((), (), s32[]{:S(2)}) async-start(), calls=%async_computation.11 | async-start | bytes 557056 | tf_op jit(solution)/shard_map/reduce_scatter | solution.py:26
  757.9 6.1 collective-permute-start.30
  788.3 6.2 collective-permute-start.35
  788.3 32.8 %collective-permute-start.42 = (f32[2,32,128]{2,1,0:T(8,128)S(1)}, f32[2,32,128]{2,1,0:T(8,128)}, u32[]{:S(2)}, u32[]{:S(2)}) collective-permute-start(f32[2,32,128]{2,1,0:T(8,128)S(1)} %collective-permute-done.41), channel_id=1, source_target_pairs={{16,0},{32,16},{48,32},{64,48},{80,64},{96,80},{112,96},{128,112},... | collective-permute-start | bytes 98312 | tf_op jit(solution)/shard_map/ppermute | solution.py:70
  794.5 31.6 %collective-permute-start.36 = (f32[2,32,128]{2,1,0:T(8,128)}, f32[2,32,128]{2,1,0:T(8,128)}, u32[]{:S(2)}, u32[]{:S(2)}) collective-permute-start(f32[2,32,128]{2,1,0:T(8,128)} %collective-permute-done.35), channel_id=1, source_target_pairs={{0,16},{16,32},{32,48},{48,64},{64,80},{80,96},{96,112},{112,128},... | collective-permute-start | bytes 98312 | tf_op jit(solution)/shard_map/ppermute | solution.py:68
  821.1 15.4 %collective-permute-start.43 = (f32[2,32,128]{2,1,0:T(8,128)}, f32[2,32,128]{2,1,0:T(8,128)}, u32[]{:S(2)}, u32[]{:S(2)}) collective-permute-start(f32[2,32,128]{2,1,0:T(8,128)} %collective-permute-done.42), channel_id=1, source_target_pairs={{16,0},{32,16},{48,32},{64,48},{80,64},{96,80},{112,96},{128,112},... | collective-permute-start | bytes 98312 | tf_op jit(solution)/shard_map/ppermute | solution.py:70
  826.1 15.2 %collective-permute-start.37 = (f32[2,32,128]{2,1,0:T(8,128)}, f32[2,32,128]{2,1,0:T(8,128)}, u32[]{:S(2)}, u32[]{:S(2)}) collective-permute-start(f32[2,32,128]{2,1,0:T(8,128)} %collective-permute-done.36), channel_id=1, source_target_pairs={{0,16},{16,32},{32,48},{48,64},{64,80},{80,96},{96,112},{112,128},... | collective-permute-start | bytes 98312 | tf_op jit(solution)/shard_map/ppermute | solution.py:68
  836.5 131.7 %reduce-scatter.17.cloned.1.call-start = ((), (), s32[]{:S(2)}) async-start(), calls=%async_computation.10 | async-start | bytes 557056 | tf_op jit(solution)/shard_map/reduce_scatter | solution.py:26
  836.5 18.6 %collective-permute-start.44 = (f32[2,32,128]{2,1,0:T(8,128)}, f32[2,32,128]{2,1,0:T(8,128)S(1)}, u32[]{:S(2)}, u32[]{:S(2)}) collective-permute-start(f32[2,32,128]{2,1,0:T(8,128)} %collective-permute-done.43), channel_id=1, source_target_pairs={{16,0},{32,16},{48,32},{64,48},{80,64},{96,80},{112,96},{128,112},... | collective-permute-start | bytes 98312 | tf_op jit(solution)/shard_map/ppermute | solution.py:70
  (49 other events, 1642.0 us)
Sparse Core Ops, SparseCore 0:
  64.4 75.8 reduce-scatter.10
  143.0 55.6 reduce-scatter.8
  472.4 73.4 reduce-scatter.14
  548.4 54.6 reduce-scatter.12
  836.6 74.4 reduce-scatter.18
  913.6 54.5 reduce-scatter.16
